TPU v7x, 256 devices: a whole 4x4x8 slice. The times are simulated.
256 devices in a mesh: row: 16 (over y_lo, x, core), col: 16 (over y_hi, z).
Axes of the slice: x: 4, y: 4 (y_hi: 2, y_lo: 2; y = y_hi * 2 + y_lo), z: 8, core: 2. Of those that a mesh axis runs over, the one named last changes fastest.
Arguments:
- val_orb: bfloat16 [64, 2048], replicated, may hold values from -6 to 6
- con_orb: bfloat16 [512, 2048], replicated, may hold values from -6 to 6
- val_energy: float32 [64], replicated, may hold values from -1.5 to -0.5
- con_energy: float32 [512], replicated, may hold values from 0.5 to 2
- points: int32 [1024], replicated, may hold values from 0 to 2047, as said below
- val_band: int32 [1048576], P(('row', 'col')), may hold values from 0 to 63
- con_band: int32 [1048576], P(('row', 'col')), may hold values from 0 to 511
- kernel: bfloat16 [1024, 1024], replicated
- trial_vecs: bfloat16 [1048576, 128], P(('row', 'col')), may hold values from -6 to 6
Outputs:
- first_degree: bfloat16 [1048576, 128], P(('row', 'col'))
- filtered: float32 [1048576, 128], P(('row', 'col'))
Inputs may be any that keep to these rules, and one draw needn't show every extreme that they name: Distinct grid points.
All inputs are finite; a program needn't handle non-finite values.
Results may differ from a plain program's by a relative error of at most 0.0042.
Values sent between devices are 32-bit elements; how exact they have to be, the bound alone decides.
A program may use at most 128 MiB of HBM per device.

v0:
```python
import jax
import jax.numpy as jnp
from jax import lax
from jax.sharding import PartitionSpec as P

filter_center = 2.25
filter_half = 1.25


def factor_rows(val_points, con_points, val_band, con_band):
    product = jnp.take(val_points, val_band, axis=0).astype(jnp.float32) * jnp.take(
        con_points, con_band, axis=0
    ).astype(jnp.float32)
    return product.astype(jnp.bfloat16)


def shards(
    val_orb, con_orb, val_energy, con_energy, points, val_band, con_band, kernel, trial_vecs
):
    val_points = jnp.take(val_orb, points, axis=1)
    con_points = jnp.take(con_orb, points, axis=1)
    energy = (jnp.take(con_energy, con_band) - jnp.take(val_energy, val_band))[:, None]
    own_rows = factor_rows(val_points, con_points, val_band, con_band)
    kernel_wide = kernel.astype(jnp.float32)
    rows_wide = own_rows.astype(jnp.float32)

    def apply_kernel(vectors):
        partial_proj = lax.dot_general(
            own_rows, vectors, (((0,), (0,)), ((), ())), preferred_element_type=jnp.float32
        )
        projected = lax.psum(partial_proj, ("row", "col"))
        mixed = jnp.dot(kernel_wide, projected, precision=lax.Precision.HIGHEST)
        return jnp.dot(rows_wide, mixed, precision=lax.Precision.HIGHEST)

    start_vecs = trial_vecs.astype(jnp.float32)
    first = ((energy - filter_center) * start_vecs + apply_kernel(trial_vecs)) / filter_half
    first_degree = first.astype(jnp.bfloat16)
    first_wide = first_degree.astype(jnp.float32)
    filtered = (
        2.0 * ((energy - filter_center) * first_wide + apply_kernel(first_degree)) / filter_half
        - start_vecs
    )
    return (first_degree, filtered)


def solution(mesh):
    placed = (
        P(),
        P(),
        P(),
        P(),
        P(),
        P(("row", "col")),
        P(("row", "col")),
        P(),
        P(("row", "col"), None),
    )
    return jax.shard_map(
        shards,
        mesh=mesh,
        in_specs=placed,
        out_specs=(P(("row", "col"), None), P(("row", "col"), None)),
        check_vma=False,
    )
```

profile of v0, /device:TPU:2, one launch (start us, length us, event | category | flops | bytes accessed | tf_op | source)
XLA Modules:
  0.0 709.2 jit_solution(5484198504451303308)
XLA Ops:
  7.2 0.8 fusion.8
  8.1 0.7 compare_and_fusion.2
  8.8 1.6 fusion.12
  10.3 2.1 fusion.9
  12.4 2.1 fusion.10
  14.5 2.1 fusion.11
  16.6 1.3 fusion.7
  17.9 1.3 compare_and_fusion
  19.2 4.0 copy.17
  23.2 5.8 gather_fusion.3
  29.0 1.2 select_bitcast_fusion
  30.2 1.5 copy.18
  31.8 1.0 copy.15
  32.8 5.2 gather_fusion.1
  38.0 1.2 select_bitcast_fusion.1
  39.1 0.1 copy.16
  39.3 18.3 %gather_fusion.4 = bf16[4096,1024]{1,0:T(8,128)(2,1)} fusion(bf16[512,1024]{1,0:T(8,128)(2,1)S(1)} %copy.18, s32[4096]{0:T(1024)S(1)} %fusion.6), kind=kCustom, calls=%fused_computation.4 | custom fusion | bytes 16793600 | tf_op jit(solution)/shard_map/jit(_take)/gather | solution.py:11
  57.5 25.9 %gather_fusion = f32[4096]{0:T(1024)S(1)} fusion(f32[512]{0:T(512)S(1)} %copy-done.1, s32[4096]{0:T(1024)S(1)} %fusion.6), kind=kCustom, calls=%fused_computation | custom fusion | bytes 49152 | tf_op jit(solution)/shard_map/jit(_take)/gather | solution.py:22
  83.5 18.3 %gather_fusion.2 = bf16[4096,1024]{1,0:T(8,128)(2,1)} fusion(bf16[64,1024]{1,0:T(8,128)(2,1)S(1)} %copy.16, s32[4096]{0:T(1024)S(1)} %copy-done.7), kind=kCustom, calls=%fused_computation.2 | custom fusion | bytes 16793600 | tf_op jit(solution)/shard_map/jit(_take)/gather | solution.py:11
  101.7 40.1 %fusion.5 = (f32[4096]{0:T(1024)S(1)}, pred[4096]{0:T(1024)(128)(4,1)S(1)}) fusion(f32[4096]{0:T(1024)S(1)} %gather_fusion, s32[4096]{0:T(1024)S(1)} %copy-done.6, f32[]{:T(128)} %bitcast, f32[]{:T(128)} %bitcast.1, f32[]{:T(128)} %bitcast.2, f32[]{:T(128)} %bitcast.3, f32[]{:T(128)} %bitcast.4, f32[]{:T(128)} %bitcast.5, f32[]{:T(128)} %bitcast.6, ...), kind=kLoop, calls=%fused_computation.19 | loop fusion | flops 581632 | bytes 69888 | tf_op jit(solution)/shard_map/sub | solution.py:36
  141.8 7.7 %multiply_convert_fusion = bf16[4096,1024]{1,0:T(8,128)(2,1)S(1)} fusion(bf16[4096,1024]{1,0:T(8,128)(2,1)} %gather_fusion.4, bf16[4096,1024]{1,0:T(8,128)(2,1)} %gather_fusion.2, pred[4096]{0:T(1024)(128)(4,1)S(1)} %get-tuple-element.3, pred[4096]{0:T(1024)(128)(4,1)S(1)} %copy-done.10), kind=kLoop, calls=%fused_computation.5 | loop fusion | flops 25165824 | bytes 25174016 | tf_op jit(solution)/shard_map/convert_element_type | solution.py:14
  149.5 3.2 copy-done.2
  152.8 3.1 fusion.13
  155.9 0.0 all-reduce.5.cloned.1.call-start
  156.0 258.4 %all-reduce.3.cloned.1.call-done = f32[1024,128]{1,0:T(8,128)} async-done(((f32[1024,128]{1,0:T(8,128)}), f32[1024,128]{1,0:T(8,128)}) %all-reduce.3.cloned.1.call-update) | async-done | bytes 524304 | tf_op jit(solution)/shard_map/psum | solution.py:31
  414.4 3.3 fusion.14
  417.8 9.3 %fusion.3 = bf16[4096,128]{1,0:T(8,128)(2,1)S(1)} fusion(bf16[4096,1024]{1,0:T(8,128)(2,1)} %copy-done.2, f32[128,1024]{1,0:T(8,128)S(1)} %fusion.14, bf16[4096,128]{1,0:T(8,128)(2,1)S(1)} %copy-done.3, f32[4096]{0:T(1024)S(1)} %get-tuple-element.2), kind=kOutput, calls=%fused_computation.11 | convolution fusion | flops 6445072384 | bytes 11026432 | tf_op jit(solution)/shard_map/dot_general | solution.py:33
  427.1 1.0 copy-done.4
  428.0 6.6 fusion.15
  434.6 254.2 %all-reduce.5.cloned.1.call-done = f32[1024,128]{1,0:T(8,128)} async-done(((f32[1024,128]{1,0:T(8,128)}), f32[1024,128]{1,0:T(8,128)}) %all-reduce.5.cloned.1.call-update) | async-done | bytes 524304 | tf_op jit(solution)/shard_map/psum | solution.py:31
  688.8 3.3 fusion.16
  692.2 10.2 %fusion.1 = f32[4096,128]{1,0:T(8,128)} fusion(bf16[4096,1024]{1,0:T(8,128)(2,1)} %copy-done.2, f32[128,1024]{1,0:T(8,128)S(1)} %fusion.16, bf16[4096,128]{1,0:T(8,128)(2,1)S(1)} %copy-done.3, bf16[4096,128]{1,0:T(8,128)(2,1)} %copy-done.4, f32[4096]{0:T(1024)S(1)} %get-tuple-element.2), kind=kOutput, calls=%fused_computation.8 | convolution fusion | flops 6445596672 | bytes 13123584 | tf_op jit(solution)/shard_map/dot_general | solution.py:33
  (26 shorter events, 0.1 us)
Async XLA Ops:
  7.2 407.3 %copy-start = (bf16[1024,1024]{1,0:T(8,128)(2,1)S(1)}, bf16[1024,1024]{1,0:T(8,128)(2,1)}, u32[]{:S(2)}) copy-start(bf16[1024,1024]{1,0:T(8,128)(2,1)} %param.16) | copy-start | bytes 6291460
  7.2 407.3 %all-reduce.3.cloned.1.call-start = ((), (), s32[]{:S(2)}) async-start(), calls=%async_computation | async-start | bytes 1048576 | tf_op jit(solution)/shard_map/psum | solution.py:31
  8.8 23.0 %copy-start.11 = (pred[1024]{0:T(1024)(128)(4,1)}, pred[1024]{0:T(1024)(128)(4,1)S(1)}, u32[]{:S(2)}) copy-start(pred[1024]{0:T(1024)(128)(4,1)S(1)} %compare_and_fusion.2) | copy-start | bytes 3076
  19.2 12.5 %copy-start.8 = (s32[4096]{0:T(1024)S(1)}, s32[4096]{0:T(1024)}, u32[]{:S(2)}) copy-start(s32[4096]{0:T(1024)} %param.15) | copy-start | bytes 49156
  19.2 12.5 %copy-start.5 = (bf16[64,2048]{1,0:T(8,128)(2,1)S(1)}, bf16[64,2048]{1,0:T(8,128)(2,1)}, u32[]{:S(2)}) copy-start(bf16[64,2048]{1,0:T(8,128)(2,1)} %param.9) | copy-start | bytes 786436
  39.2 18.3 %copy-start.1 = (f32[512]{0:T(512)S(1)}, f32[512]{0:T(512)}, u32[]{:S(2)}) copy-start(f32[512]{0:T(512)} %param.12) | copy-start | bytes 6148
  57.5 25.9 %copy-start.7 = (s32[4096]{0:T(1024)S(1)}, s32[4096]{0:T(1024)}, u32[]{:S(2)}) copy-start(s32[4096]{0:T(1024)} %fusion.7) | copy-start | bytes 49156
  83.4 18.3 %copy-start.6 = (s32[4096]{0:T(1024)S(1)}, s32[4096]{0:T(1024)}, u32[]{:S(2)}) copy-start(s32[4096]{0:T(1024)} %param.14) | copy-start | bytes 49156
  83.4 18.3 %copy-start.9 = (s32[4096]{0:T(1024)S(1)}, s32[4096]{0:T(1024)}, u32[]{:S(2)}) copy-start(s32[4096]{0:T(1024)} %param.15) | copy-start | bytes 49156
  83.4 58.3 %copy-start.10 = (pred[4096]{0:T(1024)(128)(4,1)S(1)}, pred[4096]{0:T(1024)(128)(4,1)}, u32[]{:S(2)}) copy-start(pred[4096]{0:T(1024)(128)(4,1)} %compare_and_fusion) | copy-start | bytes 12292
  141.8 11.0 %copy-start.3 = (bf16[4096,128]{1,0:T(8,128)(2,1)S(1)}, bf16[4096,128]{1,0:T(8,128)(2,1)}, u32[]{:S(2)}) copy-start(bf16[4096,128]{1,0:T(8,128)(2,1)} %param.17) | copy-start | bytes 3145732
  149.5 3.2 copy-start.2
  155.9 532.9 %all-reduce.5.cloned.1.call-start = ((), (), s32[]{:S(2)}) async-start(), calls=%async_computation.1 | async-start | bytes 1048576 | tf_op jit(solution)/shard_map/psum | solution.py:31
  427.1 1.0 copy-start.4
Sparse Core Ops, SparseCore 0:
  156.1 258.3 all-reduce.2
  434.7 254.0 all-reduce.4
where the time goes:
time: 710 us; the launch traced here: 709 us
  waiting for transfers between devices  513 us (72%)
  local copies, waits for them, and re-layouts  92.1 us (13%)
  other arithmetic  54.3 us (8%)
  matrix products  35.8 us (5%)
  between operations  14.2 us (2%)
    psum x2, waiting for transfers between devices, apply_kernel(): projected = lax.psum(partial_proj, ('row', 'col'))  513 us
    sub x1, other arithmetic, shards(): energy - filter_center  40.1 us
    gather x1, local copies, waits for them, and re-layouts, shards(): jnp.take(con_energy, con_band) - jnp.take(val_energy, val_band)  25.9 us
    dot_general x2, matrix products, apply_kernel(): return jnp.dot(rows_wide, mixed, precision=lax.Precision.HIGHEST)  19.5 us
    gather x1, local copies, waits for them, and re-layouts, factor_rows(): jnp.take(con_points, con_band, axis=0).astype(jnp.float32)  18.3 us
    gather x1, local copies, waits for them, and re-layouts, factor_rows(): jnp.take(val_points, val_band, axis=0).astype(jnp.float32)  18.3 us
  transfers between devices with their start and end apart: 2, of which 2 were waited for; matrix products, arithmetic and copies ran while one was open for 0% of the time, Pallas kernels for 0%

commit v1 on v0

--- a/solution.py
+++ b/solution.py
@@ -28,7 +28,7 @@
         partial_proj = lax.dot_general(
             own_rows, vectors, (((0,), (0,)), ((), ())), preferred_element_type=jnp.float32
         )
-        projected = lax.psum(partial_proj, ("row", "col"))
+        projected = lax.psum(lax.psum(partial_proj, "col"), "row")
         mixed = jnp.dot(kernel_wide, projected, precision=lax.Precision.HIGHEST)
         return jnp.dot(rows_wide, mixed, precision=lax.Precision.HIGHEST)
 

time: 710 us -> 765 us (1.077)
  waiting for transfers between devices: 513 us -> 563 us
    psum x2 -> x4, waiting for transfers between devices: 513 us -> 563 us  [apply_kernel(): projected = lax.psum(lax.psum(partial_proj, 'col'), 'row')]
  transfers between devices with their start and end apart: 2 -> 4, of which waited for: 2 -> 4; matrix products, arithmetic and copies ran while one was open for 0% -> 0% of each run, Pallas kernels for 0% -> 0%
where the time goes in v1:
time: 765 us; the launch traced here: 760 us
  waiting for transfers between devices  563 us (74%)
  local copies, waits for them, and re-layouts  92.1 us (12%)
  other arithmetic  54.3 us (7%)
  matrix products  35.6 us (5%)
  between operations  14 us (2%)
    psum x4, waiting for transfers between devices, apply_kernel(): projected = lax.psum(lax.psum(partial_proj, 'col'), 'row')  563 us
    sub x1, other arithmetic, shards(): energy - filter_center  40.1 us
    gather x1, local copies, waits for them, and re-layouts, shards(): jnp.take(con_energy, con_band) - jnp.take(val_energy, val_band)  25.9 us
    dot_general x2, matrix products, apply_kernel(): return jnp.dot(rows_wide, mixed, precision=lax.Precision.HIGHEST)  19.3 us
    gather x1, local copies, waits for them, and re-layouts, factor_rows(): jnp.take(con_points, con_band, axis=0).astype(jnp.float32)  18.3 us
    gather x1, local copies, waits for them, and re-layouts, factor_rows(): jnp.take(val_points, val_band, axis=0).astype(jnp.float32)  18.3 us
  transfers between devices with their start and end apart: 4, of which 4 were waited for; matrix products, arithmetic and copies ran while one was open for 0% of the time, Pallas kernels for 0%

profile of v1, /device:TPU:2, one launch (start us, length us, event | category | flops | bytes accessed | tf_op | source)
XLA Modules:
  0.0 759.8 jit_solution(16881719024077077381)
XLA Ops:
  7.2 0.8 fusion.8
  8.1 0.7 compare_and_fusion.2
  8.8 1.6 fusion.12
  10.3 2.1 fusion.9
  12.4 2.1 fusion.10
  14.5 2.1 fusion.11
  16.6 1.3 fusion.7
  17.9 1.3 compare_and_fusion
  19.2 4.0 copy.17
  23.2 5.8 gather_fusion.3
  29.0 1.2 select_bitcast_fusion
  30.2 1.5 copy.18
  31.8 1.0 copy.15
  32.8 5.2 gather_fusion.1
  38.0 1.2 select_bitcast_fusion.1
  39.3 18.3 %gather_fusion.4 = bf16[4096,1024]{1,0:T(8,128)(2,1)} fusion(bf16[512,1024]{1,0:T(8,128)(2,1)S(1)} %copy.18, s32[4096]{0:T(1024)S(1)} %fusion.6), kind=kCustom, calls=%fused_computation.4 | custom fusion | bytes 16793600 | tf_op jit(solution)/shard_map/jit(_take)/gather | solution.py:11
  57.5 25.9 %gather_fusion = f32[4096]{0:T(1024)S(1)} fusion(f32[512]{0:T(512)S(1)} %copy-done.1, s32[4096]{0:T(1024)S(1)} %fusion.6), kind=kCustom, calls=%fused_computation | custom fusion | bytes 49152 | tf_op jit(solution)/shard_map/jit(_take)/gather | solution.py:22
  83.5 18.3 %gather_fusion.2 = bf16[4096,1024]{1,0:T(8,128)(2,1)} fusion(bf16[64,1024]{1,0:T(8,128)(2,1)S(1)} %copy.16, s32[4096]{0:T(1024)S(1)} %copy-done.7), kind=kCustom, calls=%fused_computation.2 | custom fusion | bytes 16793600 | tf_op jit(solution)/shard_map/jit(_take)/gather | solution.py:11
  101.7 40.1 %fusion.5 = (f32[4096]{0:T(1024)S(1)}, pred[4096]{0:T(1024)(128)(4,1)S(1)}) fusion(f32[4096]{0:T(1024)S(1)} %gather_fusion, s32[4096]{0:T(1024)S(1)} %copy-done.6, f32[]{:T(128)} %bitcast, f32[]{:T(128)} %bitcast.1, f32[]{:T(128)} %bitcast.2, f32[]{:T(128)} %bitcast.3, f32[]{:T(128)} %bitcast.4, f32[]{:T(128)} %bitcast.5, f32[]{:T(128)} %bitcast.6, ...), kind=kLoop, calls=%fused_computation.19 | loop fusion | flops 581632 | bytes 69888 | tf_op jit(solution)/shard_map/sub | solution.py:36
  141.8 7.7 %multiply_convert_fusion = bf16[4096,1024]{1,0:T(8,128)(2,1)S(1)} fusion(bf16[4096,1024]{1,0:T(8,128)(2,1)} %gather_fusion.4, bf16[4096,1024]{1,0:T(8,128)(2,1)} %gather_fusion.2, pred[4096]{0:T(1024)(128)(4,1)S(1)} %get-tuple-element.3, pred[4096]{0:T(1024)(128)(4,1)S(1)} %copy-done.10), kind=kLoop, calls=%fused_computation.5 | loop fusion | flops 25165824 | bytes 25174016 | tf_op jit(solution)/shard_map/convert_element_type | solution.py:14
  149.5 3.2 copy-done.2
  152.8 3.1 fusion.13
  156.0 160.6 %all-reduce.5.cloned.1.call-done = f32[1024,128]{1,0:T(8,128)} async-done(((f32[1024,128]{1,0:T(8,128)}), f32[1024,128]{1,0:T(8,128)}) %all-reduce.5.cloned.1.call-update) | async-done | bytes 524304 | tf_op jit(solution)/shard_map/psum | solution.py:31
  316.8 120.4 %all-reduce.7.cloned.1.call-done = f32[1024,128]{1,0:T(8,128)} async-done(((f32[1024,128]{1,0:T(8,128)}), f32[1024,128]{1,0:T(8,128)}) %all-reduce.7.cloned.1.call-update) | async-done | bytes 524304 | tf_op jit(solution)/shard_map/psum | solution.py:31
  437.2 3.3 fusion.14
  440.5 9.1 %fusion.3 = bf16[4096,128]{1,0:T(8,128)(2,1)S(1)} fusion(bf16[4096,1024]{1,0:T(8,128)(2,1)} %copy-done.2, f32[128,1024]{1,0:T(8,128)S(1)} %fusion.14, bf16[4096,128]{1,0:T(8,128)(2,1)S(1)} %copy-done.3, f32[4096]{0:T(1024)S(1)} %get-tuple-element.2), kind=kOutput, calls=%fused_computation.11 | convolution fusion | flops 6445072384 | bytes 11026432 | tf_op jit(solution)/shard_map/dot_general | solution.py:33
  449.6 1.0 copy-done.4
  450.6 6.6 fusion.15
  457.4 161.8 %all-reduce.9.cloned.1.call-done = f32[1024,128]{1,0:T(8,128)} async-done(((f32[1024,128]{1,0:T(8,128)}), f32[1024,128]{1,0:T(8,128)}) %all-reduce.9.cloned.1.call-update) | async-done | bytes 524304 | tf_op jit(solution)/shard_map/psum | solution.py:31
  619.3 120.5 %all-reduce.11.cloned.1.call-done = f32[1024,128]{1,0:T(8,128)} async-done(((f32[1024,128]{1,0:T(8,128)}), f32[1024,128]{1,0:T(8,128)}) %all-reduce.11.cloned.1.call-update) | async-done | bytes 524304 | tf_op jit(solution)/shard_map/psum | solution.py:31
  739.7 3.3 fusion.16
  743.0 10.2 %fusion.1 = f32[4096,128]{1,0:T(8,128)} fusion(bf16[4096,1024]{1,0:T(8,128)(2,1)} %copy-done.2, f32[128,1024]{1,0:T(8,128)S(1)} %fusion.16, bf16[4096,128]{1,0:T(8,128)(2,1)S(1)} %copy-done.3, bf16[4096,128]{1,0:T(8,128)(2,1)} %copy-done.4, f32[4096]{0:T(1024)S(1)} %get-tuple-element.2), kind=kOutput, calls=%fused_computation.8 | convolution fusion | flops 6445596672 | bytes 13123584 | tf_op jit(solution)/shard_map/dot_general | solution.py:33
  (32 shorter events, 0.8 us)
Async XLA Ops:
  7.2 430.0 %copy-start = (bf16[1024,1024]{1,0:T(8,128)(2,1)S(1)}, bf16[1024,1024]{1,0:T(8,128)(2,1)}, u32[]{:S(2)}) copy-start(bf16[1024,1024]{1,0:T(8,128)(2,1)} %param.16) | copy-start | bytes 6291460
  7.2 309.4 %all-reduce.5.cloned.1.call-start = ((), (), s32[]{:S(2)}) async-start(), calls=%async_computation | async-start | bytes 1048576 | tf_op jit(solution)/shard_map/psum | solution.py:31
  8.8 23.0 %copy-start.11 = (pred[1024]{0:T(1024)(128)(4,1)}, pred[1024]{0:T(1024)(128)(4,1)S(1)}, u32[]{:S(2)}) copy-start(pred[1024]{0:T(1024)(128)(4,1)S(1)} %compare_and_fusion.2) | copy-start | bytes 3076
  19.2 12.5 %copy-start.8 = (s32[4096]{0:T(1024)S(1)}, s32[4096]{0:T(1024)}, u32[]{:S(2)}) copy-start(s32[4096]{0:T(1024)} %param.15) | copy-start | bytes 49156
  19.2 12.5 %copy-start.5 = (bf16[64,2048]{1,0:T(8,128)(2,1)S(1)}, bf16[64,2048]{1,0:T(8,128)(2,1)}, u32[]{:S(2)}) copy-start(bf16[64,2048]{1,0:T(8,128)(2,1)} %param.9) | copy-start | bytes 786436
  39.2 18.3 %copy-start.1 = (f32[512]{0:T(512)S(1)}, f32[512]{0:T(512)}, u32[]{:S(2)}) copy-start(f32[512]{0:T(512)} %param.12) | copy-start | bytes 6148
  57.5 25.9 %copy-start.7 = (s32[4096]{0:T(1024)S(1)}, s32[4096]{0:T(1024)}, u32[]{:S(2)}) copy-start(s32[4096]{0:T(1024)} %fusion.7) | copy-start | bytes 49156
  83.4 18.3 %copy-start.6 = (s32[4096]{0:T(1024)S(1)}, s32[4096]{0:T(1024)}, u32[]{:S(2)}) copy-start(s32[4096]{0:T(1024)} %param.14) | copy-start | bytes 49156
  83.4 18.3 %copy-start.9 = (s32[4096]{0:T(1024)S(1)}, s32[4096]{0:T(1024)}, u32[]{:S(2)}) copy-start(s32[4096]{0:T(1024)} %param.15) | copy-start | bytes 49156
  83.4 58.3 %copy-start.10 = (pred[4096]{0:T(1024)(128)(4,1)S(1)}, pred[4096]{0:T(1024)(128)(4,1)}, u32[]{:S(2)}) copy-start(pred[4096]{0:T(1024)(128)(4,1)} %compare_and_fusion) | copy-start | bytes 12292
  141.8 11.0 %copy-start.3 = (bf16[4096,128]{1,0:T(8,128)(2,1)S(1)}, bf16[4096,128]{1,0:T(8,128)(2,1)}, u32[]{:S(2)}) copy-start(bf16[4096,128]{1,0:T(8,128)(2,1)} %param.17) | copy-start | bytes 3145732
  149.5 3.2 copy-start.2
  155.9 281.2 %all-reduce.7.cloned.1.call-start = ((), (), s32[]{:S(2)}) async-start(), calls=%async_computation.1 | async-start | bytes 1048576 | tf_op jit(solution)/shard_map/psum | solution.py:31
  316.6 302.7 %all-reduce.9.cloned.1.call-start = ((), (), s32[]{:S(2)}) async-start(), calls=%async_computation.2 | async-start | bytes 1048576 | tf_op jit(solution)/shard_map/psum | solution.py:31
  449.6 1.0 copy-start.4
  457.2 282.5 %all-reduce.11.cloned.1.call-start = ((), (), s32[]{:S(2)}) async-start(), calls=%async_computation.3 | async-start | bytes 1048576 | tf_op jit(solution)/shard_map/psum | solution.py:31
Sparse Core Ops, SparseCore 0:
  156.1 160.4 all-reduce.4
  319.2 117.9 all-reduce.6
  457.3 161.8 all-reduce.8
  621.7 117.9 all-reduce.10
